TPU v7x, 128 devices: a whole 4x4x4 slice. The times are simulated.
128 devices in a mesh: ctx: 32 (over y_lo, z, x), ch: 4 (over y_hi, core).
Axes of the slice: x: 4, y: 4 (y_hi: 2, y_lo: 2; y = y_hi * 2 + y_lo), z: 4, core: 2. Of those that a mesh axis runs over, the one named last changes fastest.
Arguments:
- query_gate: bfloat16 [8192, 4096], P('ctx', 'ch'), may hold values from -6 to 6
- gated_value: bfloat16 [8192, 4096], P('ctx', 'ch'), may hold values from -6 to 6
- long_filter: bfloat16 [8192, 4096], P(None, 'ch'), may hold values from -0.0625 to 0.0625
- out_weight: bfloat16 [4096, 4096], P('ch'), may hold values from -0.125 to 0.125
Outputs:
- output: bfloat16 [8192, 4096], P('ctx', 'ch')
All inputs are finite; a program needn't handle non-finite values.
Results may differ from a plain program's by a relative error of at most 0.019.
Values may be sent and summed in bfloat16 or wider, within the bound.
No kernel may reach another device: no remote copies, remote signals or barrier semaphores. Data moves between devices by JAX's collectives and lax.ppermute only.
A program may use at most 128 MiB of HBM per device.

v0:
```python
import math
import jax
import jax.numpy as jnp
from jax import lax
from jax.sharding import PartitionSpec as P

SPAN = 128


def dot_high(left, right):
    return jnp.dot(left, right, precision=lax.Precision.HIGHEST, preferred_element_type=jnp.float32)


def dot_plain(left, right):
    return jnp.dot(left, right, preferred_element_type=jnp.float32)


def make_tables():
    freq_int = jnp.arange(SPAN + 1, dtype=jnp.int32)[:, None]
    half_int = jnp.arange(SPAN, dtype=jnp.int32)[None, :]
    full_int = jnp.arange(2 * SPAN, dtype=jnp.int32)[None, :]
    half_phase = (freq_int * half_int % (2 * SPAN)).astype(jnp.float32) * (math.pi / SPAN)
    full_phase = (freq_int * full_int % (2 * SPAN)).astype(jnp.float32) * (math.pi / SPAN)
    parity = jnp.where(freq_int % 2 == 0, 1.0, -1.0).astype(jnp.float32)
    x_table = jnp.concatenate([jnp.cos(half_phase), -jnp.sin(half_phase)], 0).astype(jnp.bfloat16)
    filter_table = jnp.concatenate(
        [parity * jnp.cos(full_phase), -parity * jnp.sin(full_phase)], 0
    ).astype(jnp.bfloat16)
    weights = jnp.where((freq_int == 0) | (freq_int == SPAN), 1.0, 2.0).astype(jnp.float32)
    back_phase = half_phase.T
    inverse_table = jnp.concatenate(
        [weights.T * jnp.cos(back_phase), -weights.T * jnp.sin(back_phase)], 1
    ) / (2.0 * SPAN)
    return (x_table, filter_table, inverse_table)


def filter_spectrum(long_filter, filter_table, lag_block):
    first_row = jnp.maximum(lag_block * SPAN - SPAN, 0)
    window = lax.dynamic_slice_in_dim(long_filter, first_row, 2 * SPAN, 0)
    rolled = jnp.concatenate([jnp.zeros_like(window[:SPAN]), window[:SPAN]], 0)
    window = jnp.where(lag_block == 0, rolled, window)
    return dot_plain(filter_table, window)


def complex_times(filter_spec, source_spec, axis):
    freq_rows = SPAN + 1
    filt_real = lax.slice_in_dim(filter_spec, 0, freq_rows, axis=axis)
    filt_imag = lax.slice_in_dim(filter_spec, freq_rows, 2 * freq_rows, axis=axis)
    src_real = lax.slice_in_dim(source_spec, 0, freq_rows, axis=axis)
    src_imag = lax.slice_in_dim(source_spec, freq_rows, 2 * freq_rows, axis=axis)
    return jnp.concatenate(
        [filt_real * src_real - filt_imag * src_imag, filt_real * src_imag + filt_imag * src_real],
        axis,
    )


def block_number(position, axis_count):
    device_block = position // (2 * SPAN)
    second_half = position // SPAN % 2
    return jnp.where(second_half == 0, device_block, 2 * axis_count - 1 - device_block)


def per_device(query_gate, gated_value, long_filter, out_weight):
    x_table, filter_table, inverse_table = make_tables()
    axis_count = lax.axis_size("ctx")
    my_index = lax.axis_index("ctx")
    mine_high = 2 * axis_count - 1 - my_index
    channels = gated_value.shape[1]
    freq_rows = SPAN + 1

    def pair_term(lag_block, source_spec):
        return complex_times(filter_spectrum(long_filter, filter_table, lag_block), source_spec, 0)

    start_totals = jnp.zeros((2, 2 * freq_rows, channels), jnp.float32)
    shard_rows = lax.all_gather(gated_value, "ctx", axis=0, tiled=True)
    block_count = shard_rows.shape[0] // SPAN

    def one_block(block, totals):
        block_rows = lax.dynamic_slice_in_dim(shard_rows, block * SPAN, SPAN, 0)
        source = block_number(block * SPAN, axis_count)

        def include(inner):
            source_spec = dot_plain(x_table, block_rows)
            high_part = inner[1] + pair_term(mine_high - source, source_spec)

            def add_low(low_now):
                return low_now + pair_term(my_index - source, source_spec)

            def keep_low(low_now):
                return low_now

            low_part = lax.cond(source <= my_index, add_low, keep_low, inner[0])
            return jnp.stack([low_part, high_part])

        def skip_block(inner):
            return inner

        return lax.cond(source <= mine_high, include, skip_block, totals)

    totals = lax.fori_loop(0, block_count, one_block, start_totals)
    convolved = jnp.concatenate(
        [dot_high(inverse_table, totals[0]), dot_high(inverse_table, totals[1])], 0
    )
    gated_mix = (query_gate.astype(jnp.float32) * convolved).astype(jnp.bfloat16)
    partial_sum = jnp.dot(gated_mix, out_weight, preferred_element_type=jnp.float32)
    projected = lax.psum_scatter(
        partial_sum.astype(jnp.bfloat16), "ch", scatter_dimension=1, tiled=True
    )
    return projected


def solution(mesh):
    placed = (P("ctx", "ch"), P("ctx", "ch"), P(None, "ch"), P("ch", None))
    return jax.shard_map(
        per_device, mesh=mesh, in_specs=placed, out_specs=P("ctx", "ch"), check_vma=False
    )
```

profile of v0, /device:TPU:1, one launch (start us, length us, event | category | flops | bytes accessed | tf_op | source)
XLA Modules:
  0.0 738.9 jit_solution(10108354678242873776)
XLA Ops:
  10.8 189.1 %all-gather.2.cloned.1.call-done = bf16[8192,1024]{1,0:T(8,128)(2,1)} async-done(((bf16[256,1024]{1,0:T(8,128)(2,1)}), bf16[8192,1024]{1,0:T(8,128)(2,1)}) %all-gather.2.cloned.1.call-update) | async-done | bytes 16777232 | tf_op jit(solution)/shard_map/all_gather | solution.py:75
  201.5 478.4 %while.19 = (s32[]{:T(128)}, f32[2,258,1024]{2,1,0:T(8,128)}, s32[]{:T(128)}, s32[]{:T(128)}, bf16[8192,1024]{1,0:T(8,128)(2,1)}, /*index=5*/bf16[258,128]{1,0:T...) while((s32[]{:T(128)}, f32[2,258,1024]{2,1,0:T(8,128)}, ...), condition=%wide.region_5.6_spmd, body=%wide.region_0.5_spmd.sunk | while | flops 341860384 | bytes 25414548 | solution.py:100
  201.5 10.5 %conditional.3 = (f32[2,258,1024]{2,1,0:T(8,128)}) conditional(s32[]{:T(128)} %convert_element_type.75, f32[2,258,1024]{2,1,0:T(8,128)} %get-tuple-element.461, (s32[]{:T(128)}, s32[]{:T(128)}, f32[2,258,1024]{2,1,0:T(8,128)}, s32[]{:T(128)}, pred[]{:T(512)}, /*index=5*/bf16[8192,1024]{1,0:T(8,128)(2,1)}, bf16[258,128]{1,0:T(8,128)(2,1)}, ...), branch_computations={%region_1.1_spmd, %region_2.4_spmd} | conditional | flops 341860352 | bytes 25413872 | solution.py:98
  212.0 7.4 %conditional.3 = (f32[2,258,1024]{2,1,0:T(8,128)}) conditional(s32[]{:T(128)} %convert_element_type.75, f32[2,258,1024]{2,1,0:T(8,128)} %get-tuple-element.461, (s32[]{:T(128)}, s32[]{:T(128)}, f32[2,258,1024]{2,1,0:T(8,128)}, s32[]{:T(128)}, pred[]{:T(512)}, /*index=5*/bf16[8192,1024]{1,0:T(8,128)(2,1)}, bf16[258,128]{1,0:T(8,128)(2,1)}, ...), branch_computations={%region_1.1_spmd, %region_2.4_spmd} | conditional | flops 341860352 | bytes 25413872 | solution.py:98
  219.4 7.4 %conditional.3 = (f32[2,258,1024]{2,1,0:T(8,128)}) conditional(s32[]{:T(128)} %convert_element_type.75, f32[2,258,1024]{2,1,0:T(8,128)} %get-tuple-element.461, (s32[]{:T(128)}, s32[]{:T(128)}, f32[2,258,1024]{2,1,0:T(8,128)}, s32[]{:T(128)}, pred[]{:T(512)}, /*index=5*/bf16[8192,1024]{1,0:T(8,128)(2,1)}, bf16[258,128]{1,0:T(8,128)(2,1)}, ...), branch_computations={%region_1.1_spmd, %region_2.4_spmd} | conditional | flops 341860352 | bytes 25413872 | solution.py:98
  226.8 7.4 %conditional.3 = (f32[2,258,1024]{2,1,0:T(8,128)}) conditional(s32[]{:T(128)} %convert_element_type.75, f32[2,258,1024]{2,1,0:T(8,128)} %get-tuple-element.461, (s32[]{:T(128)}, s32[]{:T(128)}, f32[2,258,1024]{2,1,0:T(8,128)}, s32[]{:T(128)}, pred[]{:T(512)}, /*index=5*/bf16[8192,1024]{1,0:T(8,128)(2,1)}, bf16[258,128]{1,0:T(8,128)(2,1)}, ...), branch_computations={%region_1.1_spmd, %region_2.4_spmd} | conditional | flops 341860352 | bytes 25413872 | solution.py:98
  234.3 7.4 %conditional.3 = (f32[2,258,1024]{2,1,0:T(8,128)}) conditional(s32[]{:T(128)} %convert_element_type.75, f32[2,258,1024]{2,1,0:T(8,128)} %get-tuple-element.461, (s32[]{:T(128)}, s32[]{:T(128)}, f32[2,258,1024]{2,1,0:T(8,128)}, s32[]{:T(128)}, pred[]{:T(512)}, /*index=5*/bf16[8192,1024]{1,0:T(8,128)(2,1)}, bf16[258,128]{1,0:T(8,128)(2,1)}, ...), branch_computations={%region_1.1_spmd, %region_2.4_spmd} | conditional | flops 341860352 | bytes 25413872 | solution.py:98
  241.7 7.4 %conditional.3 = (f32[2,258,1024]{2,1,0:T(8,128)}) conditional(s32[]{:T(128)} %convert_element_type.75, f32[2,258,1024]{2,1,0:T(8,128)} %get-tuple-element.461, (s32[]{:T(128)}, s32[]{:T(128)}, f32[2,258,1024]{2,1,0:T(8,128)}, s32[]{:T(128)}, pred[]{:T(512)}, /*index=5*/bf16[8192,1024]{1,0:T(8,128)(2,1)}, bf16[258,128]{1,0:T(8,128)(2,1)}, ...), branch_computations={%region_1.1_spmd, %region_2.4_spmd} | conditional | flops 341860352 | bytes 25413872 | solution.py:98
  249.1 7.4 %conditional.3 = (f32[2,258,1024]{2,1,0:T(8,128)}) conditional(s32[]{:T(128)} %convert_element_type.75, f32[2,258,1024]{2,1,0:T(8,128)} %get-tuple-element.461, (s32[]{:T(128)}, s32[]{:T(128)}, f32[2,258,1024]{2,1,0:T(8,128)}, s32[]{:T(128)}, pred[]{:T(512)}, /*index=5*/bf16[8192,1024]{1,0:T(8,128)(2,1)}, bf16[258,128]{1,0:T(8,128)(2,1)}, ...), branch_computations={%region_1.1_spmd, %region_2.4_spmd} | conditional | flops 341860352 | bytes 25413872 | solution.py:98
  256.6 7.4 %conditional.3 = (f32[2,258,1024]{2,1,0:T(8,128)}) conditional(s32[]{:T(128)} %convert_element_type.75, f32[2,258,1024]{2,1,0:T(8,128)} %get-tuple-element.461, (s32[]{:T(128)}, s32[]{:T(128)}, f32[2,258,1024]{2,1,0:T(8,128)}, s32[]{:T(128)}, pred[]{:T(512)}, /*index=5*/bf16[8192,1024]{1,0:T(8,128)(2,1)}, bf16[258,128]{1,0:T(8,128)(2,1)}, ...), branch_computations={%region_1.1_spmd, %region_2.4_spmd} | conditional | flops 341860352 | bytes 25413872 | solution.py:98
  264.0 7.4 %conditional.3 = (f32[2,258,1024]{2,1,0:T(8,128)}) conditional(s32[]{:T(128)} %convert_element_type.75, f32[2,258,1024]{2,1,0:T(8,128)} %get-tuple-element.461, (s32[]{:T(128)}, s32[]{:T(128)}, f32[2,258,1024]{2,1,0:T(8,128)}, s32[]{:T(128)}, pred[]{:T(512)}, /*index=5*/bf16[8192,1024]{1,0:T(8,128)(2,1)}, bf16[258,128]{1,0:T(8,128)(2,1)}, ...), branch_computations={%region_1.1_spmd, %region_2.4_spmd} | conditional | flops 341860352 | bytes 25413872 | solution.py:98
  271.4 7.4 %conditional.3 = (f32[2,258,1024]{2,1,0:T(8,128)}) conditional(s32[]{:T(128)} %convert_element_type.75, f32[2,258,1024]{2,1,0:T(8,128)} %get-tuple-element.461, (s32[]{:T(128)}, s32[]{:T(128)}, f32[2,258,1024]{2,1,0:T(8,128)}, s32[]{:T(128)}, pred[]{:T(512)}, /*index=5*/bf16[8192,1024]{1,0:T(8,128)(2,1)}, bf16[258,128]{1,0:T(8,128)(2,1)}, ...), branch_computations={%region_1.1_spmd, %region_2.4_spmd} | conditional | flops 341860352 | bytes 25413872 | solution.py:98
  278.8 7.4 %conditional.3 = (f32[2,258,1024]{2,1,0:T(8,128)}) conditional(s32[]{:T(128)} %convert_element_type.75, f32[2,258,1024]{2,1,0:T(8,128)} %get-tuple-element.461, (s32[]{:T(128)}, s32[]{:T(128)}, f32[2,258,1024]{2,1,0:T(8,128)}, s32[]{:T(128)}, pred[]{:T(512)}, /*index=5*/bf16[8192,1024]{1,0:T(8,128)(2,1)}, bf16[258,128]{1,0:T(8,128)(2,1)}, ...), branch_computations={%region_1.1_spmd, %region_2.4_spmd} | conditional | flops 341860352 | bytes 25413872 | solution.py:98
  286.3 7.4 %conditional.3 = (f32[2,258,1024]{2,1,0:T(8,128)}) conditional(s32[]{:T(128)} %convert_element_type.75, f32[2,258,1024]{2,1,0:T(8,128)} %get-tuple-element.461, (s32[]{:T(128)}, s32[]{:T(128)}, f32[2,258,1024]{2,1,0:T(8,128)}, s32[]{:T(128)}, pred[]{:T(512)}, /*index=5*/bf16[8192,1024]{1,0:T(8,128)(2,1)}, bf16[258,128]{1,0:T(8,128)(2,1)}, ...), branch_computations={%region_1.1_spmd, %region_2.4_spmd} | conditional | flops 341860352 | bytes 25413872 | solution.py:98
  293.7 7.4 %conditional.3 = (f32[2,258,1024]{2,1,0:T(8,128)}) conditional(s32[]{:T(128)} %convert_element_type.75, f32[2,258,1024]{2,1,0:T(8,128)} %get-tuple-element.461, (s32[]{:T(128)}, s32[]{:T(128)}, f32[2,258,1024]{2,1,0:T(8,128)}, s32[]{:T(128)}, pred[]{:T(512)}, /*index=5*/bf16[8192,1024]{1,0:T(8,128)(2,1)}, bf16[258,128]{1,0:T(8,128)(2,1)}, ...), branch_computations={%region_1.1_spmd, %region_2.4_spmd} | conditional | flops 341860352 | bytes 25413872 | solution.py:98
  301.1 7.4 %conditional.3 = (f32[2,258,1024]{2,1,0:T(8,128)}) conditional(s32[]{:T(128)} %convert_element_type.75, f32[2,258,1024]{2,1,0:T(8,128)} %get-tuple-element.461, (s32[]{:T(128)}, s32[]{:T(128)}, f32[2,258,1024]{2,1,0:T(8,128)}, s32[]{:T(128)}, pred[]{:T(512)}, /*index=5*/bf16[8192,1024]{1,0:T(8,128)(2,1)}, bf16[258,128]{1,0:T(8,128)(2,1)}, ...), branch_computations={%region_1.1_spmd, %region_2.4_spmd} | conditional | flops 341860352 | bytes 25413872 | solution.py:98
  308.5 7.4 %conditional.3 = (f32[2,258,1024]{2,1,0:T(8,128)}) conditional(s32[]{:T(128)} %convert_element_type.75, f32[2,258,1024]{2,1,0:T(8,128)} %get-tuple-element.461, (s32[]{:T(128)}, s32[]{:T(128)}, f32[2,258,1024]{2,1,0:T(8,128)}, s32[]{:T(128)}, pred[]{:T(512)}, /*index=5*/bf16[8192,1024]{1,0:T(8,128)(2,1)}, bf16[258,128]{1,0:T(8,128)(2,1)}, ...), branch_computations={%region_1.1_spmd, %region_2.4_spmd} | conditional | flops 341860352 | bytes 25413872 | solution.py:98
  316.0 7.4 %conditional.3 = (f32[2,258,1024]{2,1,0:T(8,128)}) conditional(s32[]{:T(128)} %convert_element_type.75, f32[2,258,1024]{2,1,0:T(8,128)} %get-tuple-element.461, (s32[]{:T(128)}, s32[]{:T(128)}, f32[2,258,1024]{2,1,0:T(8,128)}, s32[]{:T(128)}, pred[]{:T(512)}, /*index=5*/bf16[8192,1024]{1,0:T(8,128)(2,1)}, bf16[258,128]{1,0:T(8,128)(2,1)}, ...), branch_computations={%region_1.1_spmd, %region_2.4_spmd} | conditional | flops 341860352 | bytes 25413872 | solution.py:98
  323.4 7.4 %conditional.3 = (f32[2,258,1024]{2,1,0:T(8,128)}) conditional(s32[]{:T(128)} %convert_element_type.75, f32[2,258,1024]{2,1,0:T(8,128)} %get-tuple-element.461, (s32[]{:T(128)}, s32[]{:T(128)}, f32[2,258,1024]{2,1,0:T(8,128)}, s32[]{:T(128)}, pred[]{:T(512)}, /*index=5*/bf16[8192,1024]{1,0:T(8,128)(2,1)}, bf16[258,128]{1,0:T(8,128)(2,1)}, ...), branch_computations={%region_1.1_spmd, %region_2.4_spmd} | conditional | flops 341860352 | bytes 25413872 | solution.py:98
  330.8 7.4 %conditional.3 = (f32[2,258,1024]{2,1,0:T(8,128)}) conditional(s32[]{:T(128)} %convert_element_type.75, f32[2,258,1024]{2,1,0:T(8,128)} %get-tuple-element.461, (s32[]{:T(128)}, s32[]{:T(128)}, f32[2,258,1024]{2,1,0:T(8,128)}, s32[]{:T(128)}, pred[]{:T(512)}, /*index=5*/bf16[8192,1024]{1,0:T(8,128)(2,1)}, bf16[258,128]{1,0:T(8,128)(2,1)}, ...), branch_computations={%region_1.1_spmd, %region_2.4_spmd} | conditional | flops 341860352 | bytes 25413872 | solution.py:98
  338.3 7.4 %conditional.3 = (f32[2,258,1024]{2,1,0:T(8,128)}) conditional(s32[]{:T(128)} %convert_element_type.75, f32[2,258,1024]{2,1,0:T(8,128)} %get-tuple-element.461, (s32[]{:T(128)}, s32[]{:T(128)}, f32[2,258,1024]{2,1,0:T(8,128)}, s32[]{:T(128)}, pred[]{:T(512)}, /*index=5*/bf16[8192,1024]{1,0:T(8,128)(2,1)}, bf16[258,128]{1,0:T(8,128)(2,1)}, ...), branch_computations={%region_1.1_spmd, %region_2.4_spmd} | conditional | flops 341860352 | bytes 25413872 | solution.py:98
  345.7 7.4 %conditional.3 = (f32[2,258,1024]{2,1,0:T(8,128)}) conditional(s32[]{:T(128)} %convert_element_type.75, f32[2,258,1024]{2,1,0:T(8,128)} %get-tuple-element.461, (s32[]{:T(128)}, s32[]{:T(128)}, f32[2,258,1024]{2,1,0:T(8,128)}, s32[]{:T(128)}, pred[]{:T(512)}, /*index=5*/bf16[8192,1024]{1,0:T(8,128)(2,1)}, bf16[258,128]{1,0:T(8,128)(2,1)}, ...), branch_computations={%region_1.1_spmd, %region_2.4_spmd} | conditional | flops 341860352 | bytes 25413872 | solution.py:98
  353.1 7.4 %conditional.3 = (f32[2,258,1024]{2,1,0:T(8,128)}) conditional(s32[]{:T(128)} %convert_element_type.75, f32[2,258,1024]{2,1,0:T(8,128)} %get-tuple-element.461, (s32[]{:T(128)}, s32[]{:T(128)}, f32[2,258,1024]{2,1,0:T(8,128)}, s32[]{:T(128)}, pred[]{:T(512)}, /*index=5*/bf16[8192,1024]{1,0:T(8,128)(2,1)}, bf16[258,128]{1,0:T(8,128)(2,1)}, ...), branch_computations={%region_1.1_spmd, %region_2.4_spmd} | conditional | flops 341860352 | bytes 25413872 | solution.py:98
  360.5 7.4 %conditional.3 = (f32[2,258,1024]{2,1,0:T(8,128)}) conditional(s32[]{:T(128)} %convert_element_type.75, f32[2,258,1024]{2,1,0:T(8,128)} %get-tuple-element.461, (s32[]{:T(128)}, s32[]{:T(128)}, f32[2,258,1024]{2,1,0:T(8,128)}, s32[]{:T(128)}, pred[]{:T(512)}, /*index=5*/bf16[8192,1024]{1,0:T(8,128)(2,1)}, bf16[258,128]{1,0:T(8,128)(2,1)}, ...), branch_computations={%region_1.1_spmd, %region_2.4_spmd} | conditional | flops 341860352 | bytes 25413872 | solution.py:98
  368.0 7.4 %conditional.3 = (f32[2,258,1024]{2,1,0:T(8,128)}) conditional(s32[]{:T(128)} %convert_element_type.75, f32[2,258,1024]{2,1,0:T(8,128)} %get-tuple-element.461, (s32[]{:T(128)}, s32[]{:T(128)}, f32[2,258,1024]{2,1,0:T(8,128)}, s32[]{:T(128)}, pred[]{:T(512)}, /*index=5*/bf16[8192,1024]{1,0:T(8,128)(2,1)}, bf16[258,128]{1,0:T(8,128)(2,1)}, ...), branch_computations={%region_1.1_spmd, %region_2.4_spmd} | conditional | flops 341860352 | bytes 25413872 | solution.py:98
  375.4 7.4 %conditional.3 = (f32[2,258,1024]{2,1,0:T(8,128)}) conditional(s32[]{:T(128)} %convert_element_type.75, f32[2,258,1024]{2,1,0:T(8,128)} %get-tuple-element.461, (s32[]{:T(128)}, s32[]{:T(128)}, f32[2,258,1024]{2,1,0:T(8,128)}, s32[]{:T(128)}, pred[]{:T(512)}, /*index=5*/bf16[8192,1024]{1,0:T(8,128)(2,1)}, bf16[258,128]{1,0:T(8,128)(2,1)}, ...), branch_computations={%region_1.1_spmd, %region_2.4_spmd} | conditional | flops 341860352 | bytes 25413872 | solution.py:98
  382.8 7.4 %conditional.3 = (f32[2,258,1024]{2,1,0:T(8,128)}) conditional(s32[]{:T(128)} %convert_element_type.75, f32[2,258,1024]{2,1,0:T(8,128)} %get-tuple-element.461, (s32[]{:T(128)}, s32[]{:T(128)}, f32[2,258,1024]{2,1,0:T(8,128)}, s32[]{:T(128)}, pred[]{:T(512)}, /*index=5*/bf16[8192,1024]{1,0:T(8,128)(2,1)}, bf16[258,128]{1,0:T(8,128)(2,1)}, ...), branch_computations={%region_1.1_spmd, %region_2.4_spmd} | conditional | flops 341860352 | bytes 25413872 | solution.py:98
  390.2 7.4 %conditional.3 = (f32[2,258,1024]{2,1,0:T(8,128)}) conditional(s32[]{:T(128)} %convert_element_type.75, f32[2,258,1024]{2,1,0:T(8,128)} %get-tuple-element.461, (s32[]{:T(128)}, s32[]{:T(128)}, f32[2,258,1024]{2,1,0:T(8,128)}, s32[]{:T(128)}, pred[]{:T(512)}, /*index=5*/bf16[8192,1024]{1,0:T(8,128)(2,1)}, bf16[258,128]{1,0:T(8,128)(2,1)}, ...), branch_computations={%region_1.1_spmd, %region_2.4_spmd} | conditional | flops 341860352 | bytes 25413872 | solution.py:98
  397.7 7.4 %conditional.3 = (f32[2,258,1024]{2,1,0:T(8,128)}) conditional(s32[]{:T(128)} %convert_element_type.75, f32[2,258,1024]{2,1,0:T(8,128)} %get-tuple-element.461, (s32[]{:T(128)}, s32[]{:T(128)}, f32[2,258,1024]{2,1,0:T(8,128)}, s32[]{:T(128)}, pred[]{:T(512)}, /*index=5*/bf16[8192,1024]{1,0:T(8,128)(2,1)}, bf16[258,128]{1,0:T(8,128)(2,1)}, ...), branch_computations={%region_1.1_spmd, %region_2.4_spmd} | conditional | flops 341860352 | bytes 25413872 | solution.py:98
  405.1 7.4 %conditional.3 = (f32[2,258,1024]{2,1,0:T(8,128)}) conditional(s32[]{:T(128)} %convert_element_type.75, f32[2,258,1024]{2,1,0:T(8,128)} %get-tuple-element.461, (s32[]{:T(128)}, s32[]{:T(128)}, f32[2,258,1024]{2,1,0:T(8,128)}, s32[]{:T(128)}, pred[]{:T(512)}, /*index=5*/bf16[8192,1024]{1,0:T(8,128)(2,1)}, bf16[258,128]{1,0:T(8,128)(2,1)}, ...), branch_computations={%region_1.1_spmd, %region_2.4_spmd} | conditional | flops 341860352 | bytes 25413872 | solution.py:98
  412.5 7.4 %conditional.3 = (f32[2,258,1024]{2,1,0:T(8,128)}) conditional(s32[]{:T(128)} %convert_element_type.75, f32[2,258,1024]{2,1,0:T(8,128)} %get-tuple-element.461, (s32[]{:T(128)}, s32[]{:T(128)}, f32[2,258,1024]{2,1,0:T(8,128)}, s32[]{:T(128)}, pred[]{:T(512)}, /*index=5*/bf16[8192,1024]{1,0:T(8,128)(2,1)}, bf16[258,128]{1,0:T(8,128)(2,1)}, ...), branch_computations={%region_1.1_spmd, %region_2.4_spmd} | conditional | flops 341860352 | bytes 25413872 | solution.py:98
  420.0 7.4 %conditional.3 = (f32[2,258,1024]{2,1,0:T(8,128)}) conditional(s32[]{:T(128)} %convert_element_type.75, f32[2,258,1024]{2,1,0:T(8,128)} %get-tuple-element.461, (s32[]{:T(128)}, s32[]{:T(128)}, f32[2,258,1024]{2,1,0:T(8,128)}, s32[]{:T(128)}, pred[]{:T(512)}, /*index=5*/bf16[8192,1024]{1,0:T(8,128)(2,1)}, bf16[258,128]{1,0:T(8,128)(2,1)}, ...), branch_computations={%region_1.1_spmd, %region_2.4_spmd} | conditional | flops 341860352 | bytes 25413872 | solution.py:98
  427.4 7.4 %conditional.3 = (f32[2,258,1024]{2,1,0:T(8,128)}) conditional(s32[]{:T(128)} %convert_element_type.75, f32[2,258,1024]{2,1,0:T(8,128)} %get-tuple-element.461, (s32[]{:T(128)}, s32[]{:T(128)}, f32[2,258,1024]{2,1,0:T(8,128)}, s32[]{:T(128)}, pred[]{:T(512)}, /*index=5*/bf16[8192,1024]{1,0:T(8,128)(2,1)}, bf16[258,128]{1,0:T(8,128)(2,1)}, ...), branch_computations={%region_1.1_spmd, %region_2.4_spmd} | conditional | flops 341860352 | bytes 25413872 | solution.py:98
  434.8 7.4 %conditional.3 = (f32[2,258,1024]{2,1,0:T(8,128)}) conditional(s32[]{:T(128)} %convert_element_type.75, f32[2,258,1024]{2,1,0:T(8,128)} %get-tuple-element.461, (s32[]{:T(128)}, s32[]{:T(128)}, f32[2,258,1024]{2,1,0:T(8,128)}, s32[]{:T(128)}, pred[]{:T(512)}, /*index=5*/bf16[8192,1024]{1,0:T(8,128)(2,1)}, bf16[258,128]{1,0:T(8,128)(2,1)}, ...), branch_computations={%region_1.1_spmd, %region_2.4_spmd} | conditional | flops 341860352 | bytes 25413872 | solution.py:98
  442.2 7.4 %conditional.3 = (f32[2,258,1024]{2,1,0:T(8,128)}) conditional(s32[]{:T(128)} %convert_element_type.75, f32[2,258,1024]{2,1,0:T(8,128)} %get-tuple-element.461, (s32[]{:T(128)}, s32[]{:T(128)}, f32[2,258,1024]{2,1,0:T(8,128)}, s32[]{:T(128)}, pred[]{:T(512)}, /*index=5*/bf16[8192,1024]{1,0:T(8,128)(2,1)}, bf16[258,128]{1,0:T(8,128)(2,1)}, ...), branch_computations={%region_1.1_spmd, %region_2.4_spmd} | conditional | flops 341860352 | bytes 25413872 | solution.py:98
  449.7 7.4 %conditional.3 = (f32[2,258,1024]{2,1,0:T(8,128)}) conditional(s32[]{:T(128)} %convert_element_type.75, f32[2,258,1024]{2,1,0:T(8,128)} %get-tuple-element.461, (s32[]{:T(128)}, s32[]{:T(128)}, f32[2,258,1024]{2,1,0:T(8,128)}, s32[]{:T(128)}, pred[]{:T(512)}, /*index=5*/bf16[8192,1024]{1,0:T(8,128)(2,1)}, bf16[258,128]{1,0:T(8,128)(2,1)}, ...), branch_computations={%region_1.1_spmd, %region_2.4_spmd} | conditional | flops 341860352 | bytes 25413872 | solution.py:98
  457.1 7.4 %conditional.3 = (f32[2,258,1024]{2,1,0:T(8,128)}) conditional(s32[]{:T(128)} %convert_element_type.75, f32[2,258,1024]{2,1,0:T(8,128)} %get-tuple-element.461, (s32[]{:T(128)}, s32[]{:T(128)}, f32[2,258,1024]{2,1,0:T(8,128)}, s32[]{:T(128)}, pred[]{:T(512)}, /*index=5*/bf16[8192,1024]{1,0:T(8,128)(2,1)}, bf16[258,128]{1,0:T(8,128)(2,1)}, ...), branch_computations={%region_1.1_spmd, %region_2.4_spmd} | conditional | flops 341860352 | bytes 25413872 | solution.py:98
  464.5 7.4 %conditional.3 = (f32[2,258,1024]{2,1,0:T(8,128)}) conditional(s32[]{:T(128)} %convert_element_type.75, f32[2,258,1024]{2,1,0:T(8,128)} %get-tuple-element.461, (s32[]{:T(128)}, s32[]{:T(128)}, f32[2,258,1024]{2,1,0:T(8,128)}, s32[]{:T(128)}, pred[]{:T(512)}, /*index=5*/bf16[8192,1024]{1,0:T(8,128)(2,1)}, bf16[258,128]{1,0:T(8,128)(2,1)}, ...), branch_computations={%region_1.1_spmd, %region_2.4_spmd} | conditional | flops 341860352 | bytes 25413872 | solution.py:98
  471.9 7.4 %conditional.3 = (f32[2,258,1024]{2,1,0:T(8,128)}) conditional(s32[]{:T(128)} %convert_element_type.75, f32[2,258,1024]{2,1,0:T(8,128)} %get-tuple-element.461, (s32[]{:T(128)}, s32[]{:T(128)}, f32[2,258,1024]{2,1,0:T(8,128)}, s32[]{:T(128)}, pred[]{:T(512)}, /*index=5*/bf16[8192,1024]{1,0:T(8,128)(2,1)}, bf16[258,128]{1,0:T(8,128)(2,1)}, ...), branch_computations={%region_1.1_spmd, %region_2.4_spmd} | conditional | flops 341860352 | bytes 25413872 | solution.py:98
  479.4 7.4 %conditional.3 = (f32[2,258,1024]{2,1,0:T(8,128)}) conditional(s32[]{:T(128)} %convert_element_type.75, f32[2,258,1024]{2,1,0:T(8,128)} %get-tuple-element.461, (s32[]{:T(128)}, s32[]{:T(128)}, f32[2,258,1024]{2,1,0:T(8,128)}, s32[]{:T(128)}, pred[]{:T(512)}, /*index=5*/bf16[8192,1024]{1,0:T(8,128)(2,1)}, bf16[258,128]{1,0:T(8,128)(2,1)}, ...), branch_computations={%region_1.1_spmd, %region_2.4_spmd} | conditional | flops 341860352 | bytes 25413872 | solution.py:98
  486.8 7.4 %conditional.3 = (f32[2,258,1024]{2,1,0:T(8,128)}) conditional(s32[]{:T(128)} %convert_element_type.75, f32[2,258,1024]{2,1,0:T(8,128)} %get-tuple-element.461, (s32[]{:T(128)}, s32[]{:T(128)}, f32[2,258,1024]{2,1,0:T(8,128)}, s32[]{:T(128)}, pred[]{:T(512)}, /*index=5*/bf16[8192,1024]{1,0:T(8,128)(2,1)}, bf16[258,128]{1,0:T(8,128)(2,1)}, ...), branch_computations={%region_1.1_spmd, %region_2.4_spmd} | conditional | flops 341860352 | bytes 25413872 | solution.py:98
  494.2 7.4 %conditional.3 = (f32[2,258,1024]{2,1,0:T(8,128)}) conditional(s32[]{:T(128)} %convert_element_type.75, f32[2,258,1024]{2,1,0:T(8,128)} %get-tuple-element.461, (s32[]{:T(128)}, s32[]{:T(128)}, f32[2,258,1024]{2,1,0:T(8,128)}, s32[]{:T(128)}, pred[]{:T(512)}, /*index=5*/bf16[8192,1024]{1,0:T(8,128)(2,1)}, bf16[258,128]{1,0:T(8,128)(2,1)}, ...), branch_computations={%region_1.1_spmd, %region_2.4_spmd} | conditional | flops 341860352 | bytes 25413872 | solution.py:98
  501.7 7.4 %conditional.3 = (f32[2,258,1024]{2,1,0:T(8,128)}) conditional(s32[]{:T(128)} %convert_element_type.75, f32[2,258,1024]{2,1,0:T(8,128)} %get-tuple-element.461, (s32[]{:T(128)}, s32[]{:T(128)}, f32[2,258,1024]{2,1,0:T(8,128)}, s32[]{:T(128)}, pred[]{:T(512)}, /*index=5*/bf16[8192,1024]{1,0:T(8,128)(2,1)}, bf16[258,128]{1,0:T(8,128)(2,1)}, ...), branch_computations={%region_1.1_spmd, %region_2.4_spmd} | conditional | flops 341860352 | bytes 25413872 | solution.py:98
  509.1 7.4 %conditional.3 = (f32[2,258,1024]{2,1,0:T(8,128)}) conditional(s32[]{:T(128)} %convert_element_type.75, f32[2,258,1024]{2,1,0:T(8,128)} %get-tuple-element.461, (s32[]{:T(128)}, s32[]{:T(128)}, f32[2,258,1024]{2,1,0:T(8,128)}, s32[]{:T(128)}, pred[]{:T(512)}, /*index=5*/bf16[8192,1024]{1,0:T(8,128)(2,1)}, bf16[258,128]{1,0:T(8,128)(2,1)}, ...), branch_computations={%region_1.1_spmd, %region_2.4_spmd} | conditional | flops 341860352 | bytes 25413872 | solution.py:98
  516.5 7.4 %conditional.3 = (f32[2,258,1024]{2,1,0:T(8,128)}) conditional(s32[]{:T(128)} %convert_element_type.75, f32[2,258,1024]{2,1,0:T(8,128)} %get-tuple-element.461, (s32[]{:T(128)}, s32[]{:T(128)}, f32[2,258,1024]{2,1,0:T(8,128)}, s32[]{:T(128)}, pred[]{:T(512)}, /*index=5*/bf16[8192,1024]{1,0:T(8,128)(2,1)}, bf16[258,128]{1,0:T(8,128)(2,1)}, ...), branch_computations={%region_1.1_spmd, %region_2.4_spmd} | conditional | flops 341860352 | bytes 25413872 | solution.py:98
  561.1 7.4 %conditional.3 = (f32[2,258,1024]{2,1,0:T(8,128)}) conditional(s32[]{:T(128)} %convert_element_type.75, f32[2,258,1024]{2,1,0:T(8,128)} %get-tuple-element.461, (s32[]{:T(128)}, s32[]{:T(128)}, f32[2,258,1024]{2,1,0:T(8,128)}, s32[]{:T(128)}, pred[]{:T(512)}, /*index=5*/bf16[8192,1024]{1,0:T(8,128)(2,1)}, bf16[258,128]{1,0:T(8,128)(2,1)}, ...), branch_computations={%region_1.1_spmd, %region_2.4_spmd} | conditional | flops 341860352 | bytes 25413872 | solution.py:98
  613.1 7.4 %conditional.3 = (f32[2,258,1024]{2,1,0:T(8,128)}) conditional(s32[]{:T(128)} %convert_element_type.75, f32[2,258,1024]{2,1,0:T(8,128)} %get-tuple-element.461, (s32[]{:T(128)}, s32[]{:T(128)}, f32[2,258,1024]{2,1,0:T(8,128)}, s32[]{:T(128)}, pred[]{:T(512)}, /*index=5*/bf16[8192,1024]{1,0:T(8,128)(2,1)}, bf16[258,128]{1,0:T(8,128)(2,1)}, ...), branch_computations={%region_1.1_spmd, %region_2.4_spmd} | conditional | flops 341860352 | bytes 25413872 | solution.py:98
  691.9 40.1 %reduce-scatter.2.cloned.1.call-done = bf16[256,1024]{1,0:T(8,128)(2,1)} async-done(((bf16[256,4096]{1,0:T(8,128)(2,1)}), bf16[256,1024]{1,0:T(8,128)(2,1)}) %reduce-scatter.2.cloned.1.call-update) | async-done | bytes 524304 | tf_op jit(solution)/shard_map/reduce_scatter | solution.py:106
  (490 shorter events, 636.9 us)
Async XLA Ops:
  6.5 193.3 %all-gather.2.cloned.1.call-start = ((), (), s32[]{:S(2)}) async-start(), calls=%async_computation.1 | async-start | bytes 17301504 | tf_op jit(solution)/shard_map/all_gather | solution.py:75
  7.3 724.8 %reduce-scatter.2.cloned.1.call-start = ((), (), s32[]{:S(2)}) async-start(), calls=%async_computation.2 | async-start | bytes 2621440 | tf_op jit(solution)/shard_map/reduce_scatter | solution.py:106
  679.9 4.9 copy-start
Sparse Core Ops, SparseCore 0:
  9.0 190.8 all-gather.1
  692.1 39.9 reduce-scatter.1
where the time goes:
time: 746 us; the launch traced here: 739 us
  other arithmetic  237 us (32%)
  waiting for transfers between devices  230 us (31%)
  matrix products  186 us (25%)
  local copies, waits for them, and re-layouts  68.5 us (9%)
  between operations  13.5 us (2%)
    all_gather x1, waiting for transfers between devices, per_device(): shard_rows = lax.all_gather(gated_value, 'ctx', axis=0, tiled=True)  189 us
    dot_general x129, matrix products, dot_plain(): return jnp.dot(left, right, preferred_element_type=jnp.float32)  174 us
    squeeze x64, other arithmetic, include(): low_part = lax.cond(source <= my_index, add_low, keep_low, inner[0])  120 us
    another operation x65, other arithmetic, include(): return jnp.stack([low_part, high_part])  97 us
    slice x65, local copies, waits for them, and re-layouts, filter_spectrum(): rolled = jnp.concatenate([jnp.zeros_like(window[:SPAN]), window[:SPAN]], 0)  66.8 us
    reduce_scatter x1, waiting for transfers between devices, per_device(): lax.psum_scatter(partial_sum.astype(jnp.bfloat16), 'ch', scatter_dimensio...  40.1 us
    concatenate x64, other arithmetic, complex_times(): jnp.concatenate([filt_real * src_real - filt_imag * src_imag, filt_real *...  15.8 us
  transfers between devices with their start and end apart: 2, of which 2 were waited for; matrix products, arithmetic and copies ran while one was open for 0% of the time, Pallas kernels for 0%

commit v1 on v0

--- a/solution.py
+++ b/solution.py
@@ -72,7 +72,9 @@
         return complex_times(filter_spectrum(long_filter, filter_table, lag_block), source_spec, 0)
 
     start_totals = jnp.zeros((2, 2 * freq_rows, channels), jnp.float32)
-    shard_rows = lax.all_gather(gated_value, "ctx", axis=0, tiled=True)
+    shard_rows = jnp.concatenate(
+        lax.all_to_all(jnp.stack([gated_value] * lax.axis_size("ctx")), "ctx", 0, 0), axis=0
+    )
     block_count = shard_rows.shape[0] // SPAN
 
     def one_block(block, totals):

time: 746 us -> 823 us (1.10)
  waiting for transfers between devices: 230 us -> 292 us
  starting transfers between devices: 0.04 us -> 9.89 us
    all_to_all x0 -> x1, waiting for transfers between devices: none -> 256 us  [per_device(): lax.all_to_all(jnp.stack([gated_value] * lax.axis_size('ctx')), 'ctx', 0, 0)]
    all_gather x1 -> x0, waiting for transfers between devices: 189 us -> none  [per_device(): shard_rows = lax.all_gather(gated_value, 'ctx', axis=0, tiled=True)]
    all_to_all x0 -> x1, starting transfers between devices: none -> 9.85 us  [per_device(): lax.all_to_all(jnp.stack([gated_value] * lax.axis_size('ctx')), 'ctx', 0, 0)]
where the time goes in v1:
time: 823 us; the launch traced here: 816 us
  waiting for transfers between devices  292 us (35%)
  other arithmetic  236 us (29%)
  matrix products  186 us (23%)
  local copies, waits for them, and re-layouts  74.7 us (9%)
  between operations  13.5 us (2%)
  starting transfers between devices  9.89 us (1%)
    all_to_all x1, waiting for transfers between devices, per_device(): lax.all_to_all(jnp.stack([gated_value] * lax.axis_size('ctx')), 'ctx', 0, 0)  256 us
    dot_general x129, matrix products, dot_plain(): return jnp.dot(left, right, preferred_element_type=jnp.float32)  174 us
    squeeze x64, other arithmetic, include(): low_part = lax.cond(source <= my_index, add_low, keep_low, inner[0])  120 us
    another operation x65, other arithmetic, include(): return jnp.stack([low_part, high_part])  96.7 us
    slice x65, local copies, waits for them, and re-layouts, filter_spectrum(): rolled = jnp.concatenate([jnp.zeros_like(window[:SPAN]), window[:SPAN]], 0)  66.3 us
    reduce_scatter x1, waiting for transfers between devices, per_device(): lax.psum_scatter(partial_sum.astype(jnp.bfloat16), 'ch', scatter_dimensio...  35.8 us
  transfers between devices with their start and end apart: 2, of which 2 were waited for; matrix products, arithmetic and copies ran while one was open for 0% of the time, Pallas kernels for 0%

profile of v1, /device:TPU:1, one launch (start us, length us, event | category | flops | bytes accessed | tf_op | source)
XLA Modules:
  0.0 816.3 jit_solution(7366283177940545944)
XLA Ops:
  13.3 9.9 %all-to-all-start = ((bf16[32,256,1024]{2,1,0:T(8,128)(2,1)}), bf16[32,256,1024]{2,1,0:T(8,128)(2,1)}, u32[]{:S(2)}, u32[]{:S(2)}) async-start(bf16[32,256,1024]{2,1,0:T(8,128)(2,1)} %stack.14), calls=%async_computation | async-start | bytes 33554432 | tf_op jit(solution)/shard_map/all_to_all | solution.py:76
  26.7 256.3 %all-to-all-done = bf16[32,256,1024]{2,1,0:T(8,128)(2,1)} async-done(((bf16[32,256,1024]{2,1,0:T(8,128)(2,1)}), bf16[32,256,1024]{2,1,0:T(8,128)(2,1)}, u32[]{:S(2)}, u32[]{:S(2)}) %all-to-all-start) | async-done | bytes 16777248 | tf_op jit(solution)/shard_map/all_to_all | solution.py:76
  284.6 477.0 %while.19 = (s32[]{:T(128)}, f32[2,258,1024]{2,1,0:T(8,128)}, s32[]{:T(128)}, s32[]{:T(128)}, bf16[8192,1024]{1,0:T(8,128)(2,1)}, /*index=5*/bf16[258,128]{1,0:T...) while((s32[]{:T(128)}, f32[2,258,1024]{2,1,0:T(8,128)}, ...), condition=%wide.region_5.6_spmd, body=%wide.region_0.5_spmd.sunk | while | flops 341860384 | bytes 25414540 | solution.py:102
  284.6 10.5 %conditional.3 = (f32[2,258,1024]{2,1,0:T(8,128)}) conditional(s32[]{:T(128)} %convert_element_type.75, f32[2,258,1024]{2,1,0:T(8,128)} %get-tuple-element.461, (s32[]{:T(128)}, s32[]{:T(128)}, f32[2,258,1024]{2,1,0:T(8,128)}, s32[]{:T(128)}, pred[]{:T(512)}, /*index=5*/bf16[8192,1024]{1,0:T(8,128)(2,1)}, bf16[258,128]{1,0:T(8,128)(2,1)}, ...), branch_computations={%region_1.1_spmd, %region_2.4_spmd} | conditional | flops 341860352 | bytes 25413872 | solution.py:100
  295.1 7.4 conditional.3
  302.5 7.4 conditional.3
  309.9 7.4 conditional.3
  324.8 7.4 conditional.3
  332.2 7.4 conditional.3
  347.0 7.4 conditional.3
  354.4 7.4 conditional.3
  369.2 7.4 conditional.3
  376.6 7.4 conditional.3
  391.4 7.4 conditional.3
  398.8 7.4 conditional.3
  413.6 7.4 conditional.3
  421.0 7.4 conditional.3
  435.8 7.4 conditional.3
  443.2 7.4 conditional.3
  458.0 7.4 conditional.3
  465.4 7.4 conditional.3
  480.3 7.4 conditional.3
  487.7 7.4 conditional.3
  502.5 7.4 conditional.3
  509.9 7.4 conditional.3
  524.7 7.4 conditional.3
  532.1 7.4 conditional.3
  546.9 7.4 conditional.3
  554.3 7.4 conditional.3
  569.1 7.4 conditional.3
  576.5 7.4 conditional.3
  591.3 7.4 conditional.3
  598.7 7.4 conditional.3
  613.5 7.4 conditional.3
  621.0 7.4 conditional.3
  635.8 7.4 conditional.3
  643.2 7.4 conditional.3
  658.0 7.4 conditional.3
  665.4 7.4 conditional.3
  680.2 7.4 conditional.3
  687.6 7.4 conditional.3
  702.4 7.4 conditional.3
  709.8 7.4 conditional.3
  724.6 7.4 conditional.3
  732.0 7.4 conditional.3
  746.8 7.4 conditional.3
  754.2 7.4 conditional.3
  773.7 35.8 %reduce-scatter.2.cloned.1.call-done = bf16[256,1024]{1,0:T(8,128)(2,1)} async-done(((bf16[256,4096]{1,0:T(8,128)(2,1)}), bf16[256,1024]{1,0:T(8,128)(2,1)}) %reduce-scatter.2.cloned.1.call-update) | async-done | bytes 524304 | tf_op jit(solution)/shard_map/reduce_scatter | solution.py:108
  (490 shorter events, 648.2 us)
Async XLA Ops:
  13.3 269.7 %all-to-all-start = ((bf16[32,256,1024]{2,1,0:T(8,128)(2,1)}), bf16[32,256,1024]{2,1,0:T(8,128)(2,1)}, u32[]{:S(2)}, u32[]{:S(2)}) async-start(bf16[32,256,1024]{2,1,0:T(8,128)(2,1)} %stack.14), calls=%async_computation | async-start | bytes 33554432 | tf_op jit(solution)/shard_map/all_to_all | solution.py:76
  23.2 786.3 %reduce-scatter.2.cloned.1.call-start = ((), (), s32[]{:S(2)}) async-start(), calls=%async_computation.2 | async-start | bytes 2621440 | tf_op jit(solution)/shard_map/reduce_scatter | solution.py:108
  761.6 4.9 copy-start
Sparse Core Ops, SparseCore 0:
  773.8 35.6 reduce-scatter.1
